TPU v7x, 32 devices: a whole 2x2x4 slice. The times are simulated.
32 devices in a mesh: groups: 1, kcol: 16 (over z, y, x), qrow: 2 (over core).
Axes of the slice: x: 2, y: 2, z: 4, core: 2. Of those that a mesh axis runs over, the one named last changes fastest.
Arguments:
- queries: bfloat16 [128, 1024], P(('groups', 'kcol', 'qrow')), may hold values from -120 to 120
- key_value: bfloat16 [24576, 256], P(('groups', 'kcol')), may hold values from -6 to 6
- block_lists: int32 [1, 64], P('groups'), may hold values from 0 to 191, as said below
Outputs:
- attended: bfloat16 [128, 1024], P(('groups', 'kcol', 'qrow'))
Inputs may be any that keep to these rules, and one draw needn't show every extreme that they name: `block_lists`: row i names 64 distinct key blocks, none after block 191 + i (the block that holds query block i); it always names that block, the 11 blocks just before it, and block 0.
All inputs are finite; a program needn't handle non-finite values.
Results may differ from a plain program's by a relative error of at most 0.0065.
Values may be sent and summed in bfloat16 or wider, within the bound.
No kernel may reach another device: no remote copies, remote signals or barrier semaphores. Data moves between devices by JAX's collectives and lax.ppermute only.
A program may use at most 128 MiB of HBM per device.

v0:
```python
import math
import jax
import jax.numpy as jnp
from jax import lax
from jax.sharding import PartitionSpec as P

BLK = 128
masked_score = -1e30


def combined_all(part, axis, combine):
    gathered = jax.tree.map(lambda a: lax.all_gather(a, axis), part)

    def take(source):
        return jax.tree.map(lambda a: lax.dynamic_index_in_dim(a, source, 0, False), gathered)

    return lax.fori_loop(
        1, lax.axis_size(axis), lambda source, state: combine(state, take(source)), take(0)
    )


def partial_softmax(query_tile, key_rows, value_rows, visible):
    score_scale = 1.0 / math.sqrt(key_rows.shape[1])
    scores = (
        jnp.einsum("thd,kd->htk", query_tile, key_rows, preferred_element_type=jnp.float32)
        * score_scale
    )
    scores = jnp.where(visible[None], scores, masked_score)
    row_max = jnp.max(scores, axis=-1)
    weights = jnp.where(visible[None], jnp.exp(scores - row_max[..., None]), 0.0)
    row_total = jnp.sum(weights, axis=-1)
    numerator = jnp.einsum(
        "htk,kd->thd", weights.astype(jnp.bfloat16), value_rows, preferred_element_type=jnp.float32
    )
    return (jnp.transpose(row_max), jnp.transpose(row_total), numerator)


def combine_partials(left_part, right_part):
    max_left, total_left, numer_left = left_part
    max_right, total_right, numer_right = right_part
    row_max = jnp.maximum(max_left, max_right)
    scale_left = jnp.exp(max_left - row_max)
    scale_right = jnp.exp(max_right - row_max)
    return (
        row_max,
        total_left * scale_left + total_right * scale_right,
        numer_left * scale_left[..., None] + numer_right * scale_right[..., None],
    )


def per_device(queries, key_value, block_lists):
    column_count = lax.axis_size("kcol")
    column = lax.axis_index("kcol")
    row_count = lax.axis_size("qrow")
    row_index = lax.axis_index("qrow")
    tok_dev = queries.shape[0]
    feature_count = queries.shape[1]
    head_dim = key_value.shape[1] // 2
    head_count = feature_count // head_dim
    stored = key_value.shape[0] // BLK
    all_blocks = stored * column_count
    gathered = lax.all_gather(queries, "kcol", axis=0, tiled=True)
    gathered_rows = gathered.shape[0]
    tile_rows = BLK // row_count
    query_blocks = gathered_rows // tile_rows
    offset = (all_blocks - query_blocks) * BLK
    gather_pos = jnp.arange(gathered_rows, dtype=jnp.int32)
    token_index = (gather_pos // tok_dev * row_count + row_index) * tok_dev + gather_pos % tok_dev
    query_pos = (offset + token_index).reshape(query_blocks, tile_rows)
    query_tiles = gathered.reshape(query_blocks, tile_rows, head_count, head_dim)
    block_ids = column * stored + jnp.arange(stored, dtype=jnp.int32)
    key_pos = column * stored * BLK + jnp.arange(stored * BLK, dtype=jnp.int32)
    key_rows = key_value[:, :head_dim]
    value_rows = key_value[:, head_dim:]

    def one_block(inputs):
        query_tile, positions, listed = inputs
        listed_here = jnp.any(listed[:, None] == block_ids[None, :], axis=0)
        usable = jnp.repeat(listed_here, BLK, total_repeat_length=stored * BLK)
        visible = usable[None, :] & (key_pos[None, :] <= positions[:, None])
        return partial_softmax(query_tile, key_rows, value_rows, visible)

    row_max, row_total, numerator = lax.map(one_block, (query_tiles, query_pos, block_lists))
    row_max = row_max.reshape(gathered_rows, head_count)
    row_total = row_total.reshape(gathered_rows, head_count)
    numerator = numerator.reshape(gathered_rows, head_count, head_dim)
    merged = combined_all((row_max, row_total, numerator), "kcol", combine_partials)
    first_row = column * tok_dev
    summed_total = lax.dynamic_slice_in_dim(merged[1], first_row, tok_dev, 0)
    summed_numer = lax.dynamic_slice_in_dim(merged[2], first_row, tok_dev, 0)
    attended = summed_numer / summed_total[..., None]
    return attended.reshape(tok_dev, feature_count).astype(jnp.bfloat16)


def solution(mesh):
    placed = (P(("groups", "kcol", "qrow"), None), P(("groups", "kcol"), None), P("groups", None))
    return jax.shard_map(
        per_device,
        mesh=mesh,
        in_specs=placed,
        out_specs=P(("groups", "kcol", "qrow"), None),
        check_vma=False,
    )
```

profile of v0, /device:TPU:0, one launch (start us, length us, event | category | flops | bytes accessed | tf_op | source)
XLA Modules:
  0.0 169.5 jit_solution(10916630586948243898)
XLA Ops:
  8.1 43.3 %all-gather.3 = bf16[16,4,1024]{2,1,0:T(4,128)(2,1)S(1)} all-gather(bf16[1,4,1024]{2,1,0:T(4,128)(2,1)} %bitcast.104), channel_id=1, replica_groups=mesh['groups'=1,'kcol'=16,'qrow'=2] {'kcol'}, dimensions={0}, use_global_device_ids=true | all-gather | bytes 139264 | tf_op jit(solution)/shard_map/all_gather | solution.py:62
  51.5 4.5 %select_reduce_fusion = (pred[1536]{0:T(1024)(128)(4,1)S(1)}, pred[1536]{0:T(1024)(128)(4,1)S(1)}, pred[1536]{0:T(1024)(128)(4,1)S(1)}, pred[1536]{0:T(1024)(128...) fusion(pred[]{:T(512)} %bitcast.11, pred[]{:T(512)} %bitcast.12, pred[]{:T(512)} %bitcast.13, ...), kind=kLoop, calls=%fused_computation.28 | loop fusion | flops 29184 | bytes 21511 | tf_op jit(solution)/shard_map/while/body/eval_jaxpr/jit(_take)/gather | solution.py:79
  56.0 3.2 %fusion.29 = pred[1536]{0:T(1024)(128)(4,1)S(1)} fusion(pred[1536]{0:T(1024)(128)(4,1)S(1)} %get-tuple-element.267, pred[1536]{0:T(1024)(128)(4,1)S(1)} %get-tuple-element.266, pred[1536]{0:T(1024)(128)(4,1)S(1)} %get-tuple-element.265, pred[1536]{0:T(1024)(128)(4,1)S(1)} %get-tuple-element.263, pred[1536]{0:T(1024)(128)(4,1)S(1)} %get-tuple-element.264, ...), kind=kLoop, calls=%fused_computation.47 | loop fusion | flops 21504 | bytes 10757 | tf_op jit(solution)/shard_map/while/body/eval_jaxpr/jit(_take)/select_n | solution.py:79
  59.4 1.7 %fusion.38 = (f32[8,64]{1,0:T(8,128)S(1)}, f32[8,64,1536]{2,1,0:T(8,128)S(1)}) fusion(bf16[64,8,128]{2,1,0:T(8,128)(2,1)S(1)} %squeeze.51, bf16[1536,256]{1,0:T(8,128)(2,1)} %param.8, pred[64,1536]{1,0:T(8,128)(4,1)S(1)} %compare_and_fusion), kind=kOutput, calls=%fused_computation.65 | convolution fusion | flops 203685376 | bytes 3770368 | tf_op jit(solution)/shard_map/while/body/eval_jaxpr/thd,kd->htk/dot_general | solution.py:25
  61.1 1.3 fusion.13
  63.2 36.2 %all-gather.5 = f32[16,64,8]{1,2,0:T(8,128)S(1)} all-gather(f32[1,64,8]{1,2,0:T(8,128)S(1)} %bitcast.103), channel_id=3, replica_groups=mesh['groups'=1,'kcol'=16,'qrow'=2] {'kcol'}, dimensions={0}, use_global_device_ids=true | all-gather | bytes 34816 | tf_op jit(solution)/shard_map/all_gather | solution.py:12
  99.4 39.0 %all-gather.4 = f32[16,64,8]{1,2,0:T(8,128)S(1)} all-gather(f32[1,64,8]{1,2,0:T(8,128)S(1)} %bitcast.102), channel_id=2, replica_groups=mesh['groups'=1,'kcol'=16,'qrow'=2] {'kcol'}, dimensions={0}, use_global_device_ids=true | all-gather | bytes 34816 | tf_op jit(solution)/shard_map/all_gather | solution.py:12
  138.4 1.0 slice.53
  139.6 22.3 %while.26 = (s32[]{:T(128)}, f32[64,8]{0,1:T(8,128)S(1)}, f32[64,8]{0,1:T(8,128)S(1)}, f32[64,8,128]{2,1,0:T(8,128)S(1)}, f32[16,64,8]{1,2,0:T(8,128)S(1)}, /*in...) while((s32[]{:T(128)}, f32[64,8]{0,1:T(8,128)S(1)}, ...), condition=%wide.region_4.5_spmd, body=%wide.region_3.4_spmd.sunk | while | flops 199685 | bytes 1339535 | solution.py:17
  139.8 1.0 constant_dynamic-slice_fusion.3
  141.3 1.0 constant_dynamic-slice_fusion.3
  142.7 1.0 constant_dynamic-slice_fusion.3
  144.2 1.0 constant_dynamic-slice_fusion.3
  145.7 1.0 constant_dynamic-slice_fusion.3
  147.2 1.0 constant_dynamic-slice_fusion.3
  148.7 1.0 constant_dynamic-slice_fusion.3
  150.2 1.0 constant_dynamic-slice_fusion.3
  151.7 1.0 constant_dynamic-slice_fusion.3
  153.1 1.0 constant_dynamic-slice_fusion.3
  154.6 1.0 constant_dynamic-slice_fusion.3
  156.1 1.0 constant_dynamic-slice_fusion.3
  157.6 1.0 constant_dynamic-slice_fusion.3
  159.1 1.0 constant_dynamic-slice_fusion.3
  160.6 1.0 constant_dynamic-slice_fusion.3
  (81 shorter events, 10.8 us)
Async XLA Ops:
  6.5 131.9 %all-gather.8.cloned.1.call-start = ((), (), s32[]{:S(2)}) async-start(), calls=%async_computation | async-start | bytes 4456448 | tf_op jit(solution)/shard_map/all_gather | solution.py:12
  51.5 9.6 %copy-start = (bf16[1536,256]{1,0:T(8,128)(2,1)S(1)}, bf16[1536,256]{1,0:T(8,128)(2,1)}, u32[]{:S(2)}) copy-start(bf16[1536,256]{1,0:T(8,128)(2,1)} %param.8) | copy-start | bytes 2359300
Sparse Core Ops, SparseCore 0:
  62.6 72.8 all-gather.7
where the time goes:
time: 170 us
  blocking collectives  119 us (70%)
  local copies, waits for them, and re-layouts  19.7 us (12%)
  other arithmetic  14.2 us (8%)
  between operations  13.5 us (8%)
  matrix products  3.06 us (2%)
    all_gather x2, blocking collectives, combined_all(): gathered = jax.tree.map(lambda a: lax.all_gather(a, axis), part)  75.2 us
    all_gather x1, blocking collectives, per_device(): gathered = lax.all_gather(queries, 'kcol', axis=0, tiled=True)  43.3 us
    dynamic_slice x18, local copies, waits for them, and re-layouts, take(): lax.dynamic_index_in_dim(a, source, 0, False)  15.5 us
    gather x1, other arithmetic, one_block(): usable = jnp.repeat(listed_here, BLK, total_repeat_length=stored * BLK)  4.49 us
    add x15, other arithmetic, combine_partials(): numer_left * scale_left[..., None] + numer_right * scale_right[..., None]  4.46 us
  transfers between devices with their start and end apart: 1, of which 0 were waited for; matrix products, arithmetic and copies ran while one was open for 0% of the time, Pallas kernels for 0%

commit v1 on v0

--- a/solution.py
+++ b/solution.py
@@ -59,7 +59,12 @@
     head_count = feature_count // head_dim
     stored = key_value.shape[0] // BLK
     all_blocks = stored * column_count
-    gathered = lax.all_gather(queries, "kcol", axis=0, tiled=True)
+    ring = [queries]
+    for hop in range(15):
+        ring.append(lax.ppermute(ring[-1], "kcol", [(dev, (dev + 1) % 16) for dev in range(16)]))
+    gathered = jnp.roll(
+        jnp.concatenate(ring[::-1], axis=0), (lax.axis_index("kcol") + 1) * ring[0].shape[0], axis=0
+    )
     gathered_rows = gathered.shape[0]
     tile_rows = BLK // row_count
     query_blocks = gathered_rows // tile_rows

time: 170 us -> 230 us (1.35)
  waiting for transfers between devices: 0.02 us -> 97.9 us
  blocking collectives: 119 us -> 75.4 us
  other arithmetic: 14.2 us -> 28 us
  local copies, waits for them, and re-layouts: 19.7 us -> 7.07 us
  starting transfers between devices: 0.01 us -> 3.01 us
    ppermute x0 -> x15, waiting for transfers between devices: none -> 97.9 us  [per_device(): lax.ppermute(ring[-1], 'kcol', [(dev, (dev + 1) % 16) for dev in range(16)])]
    all_gather x1 -> x0, blocking collectives: 43.3 us -> none  [per_device(): gathered = lax.all_gather(queries, 'kcol', axis=0, tiled=True)]
    dynamic_slice x18 -> x3, local copies, waits for them, and re-layouts: 15.5 us -> 0.97 us  [take(): lax.dynamic_index_in_dim(a, source, 0, False)]
    add x15, other arithmetic: 4.46 us -> 18.1 us  [combine_partials(): numer_left * scale_left[..., None] + numer_right * scale_right[..., None]]
    ppermute x0 -> x15, starting transfers between devices: none -> 3 us  [per_device(): lax.ppermute(ring[-1], 'kcol', [(dev, (dev + 1) % 16) for dev in range(16)])]
  transfers between devices with their start and end apart: 1 -> 16, of which waited for: 0 -> 15; matrix products, arithmetic and copies ran while one was open for 0% -> 5% of each run, Pallas kernels for 0% -> 0%
where the time goes in v1:
time: 230 us; the launch traced here: 229 us
  waiting for transfers between devices  97.9 us (43%)
  blocking collectives  75.4 us (33%)
  other arithmetic  28 us (12%)
  between operations  13.5 us (6%)
  local copies, waits for them, and re-layouts  7.07 us (3%)
  matrix products  3.45 us (2%)
  starting transfers between devices  3.01 us (1%)
    ppermute x15, waiting for transfers between devices, per_device(): lax.ppermute(ring[-1], 'kcol', [(dev, (dev + 1) % 16) for dev in range(16)])  97.9 us
    all_gather x2, blocking collectives, combined_all(): gathered = jax.tree.map(lambda a: lax.all_gather(a, axis), part)  75.4 us
    add x15, other arithmetic, combine_partials(): numer_left * scale_left[..., None] + numer_right * scale_right[..., None]  18.1 us
  transfers between devices with their start and end apart: 16, of which 15 were waited for; matrix products, arithmetic and copies ran while one was open for 5% of the time, Pallas kernels for 0%

profile of v1, /device:TPU:0, one launch (start us, length us, event | category | flops | bytes accessed | tf_op | source)
XLA Modules:
  0.0 228.7 jit_solution(2490018167699995257)
XLA Ops:
  6.5 3.0 %collective-permute-start = (bf16[4,1024]{1,0:T(4,128)(2,1)}, bf16[4,1024]{1,0:T(4,128)(2,1)S(1)}, u32[]{:S(2)}, u32[]{:S(2)}) collective-permute-start(bf16[4,1024]{1,0:T(4,128)(2,1)} %param.7), channel_id=1, source_target_pairs={{0,2},{2,4},{4,6},{6,8},{8,10},{10,12},{12,14},{14,16},{16,18},{18... | collective-permute-start | bytes 24584 | tf_op jit(solution)/shard_map/ppermute | solution.py:64
  9.5 5.8 %collective-permute-done = bf16[4,1024]{1,0:T(4,128)(2,1)S(1)} collective-permute-done((bf16[4,1024]{1,0:T(4,128)(2,1)}, bf16[4,1024]{1,0:T(4,128)(2,1)S(1)}, u32[]{:S(2)}, u32[]{:S(2)}) %collective-permute-start) | collective-permute-done | bytes 8224 | tf_op jit(solution)/shard_map/ppermute | solution.py:64
  15.3 7.2 %collective-permute-done.1 = bf16[4,1024]{1,0:T(4,128)(2,1)S(1)} collective-permute-done((bf16[4,1024]{1,0:T(4,128)(2,1)S(1)}, bf16[4,1024]{1,0:T(4,128)(2,1)S(1)}, u32[]{:S(2)}, u32[]{:S(2)}) %collective-permute-start.1) | collective-permute-done | bytes 8224 | tf_op jit(solution)/shard_map/ppermute | solution.py:64
  22.6 7.2 %collective-permute-done.2 = bf16[4,1024]{1,0:T(4,128)(2,1)S(1)} collective-permute-done((bf16[4,1024]{1,0:T(4,128)(2,1)S(1)}, bf16[4,1024]{1,0:T(4,128)(2,1)S(1)}, u32[]{:S(2)}, u32[]{:S(2)}) %collective-permute-start.2) | collective-permute-done | bytes 8224 | tf_op jit(solution)/shard_map/ppermute | solution.py:64
  29.8 7.2 %collective-permute-done.3 = bf16[4,1024]{1,0:T(4,128)(2,1)S(1)} collective-permute-done((bf16[4,1024]{1,0:T(4,128)(2,1)S(1)}, bf16[4,1024]{1,0:T(4,128)(2,1)S(1)}, u32[]{:S(2)}, u32[]{:S(2)}) %collective-permute-start.3) | collective-permute-done | bytes 8224 | tf_op jit(solution)/shard_map/ppermute | solution.py:64
  37.1 7.2 %collective-permute-done.4 = bf16[4,1024]{1,0:T(4,128)(2,1)S(1)} collective-permute-done((bf16[4,1024]{1,0:T(4,128)(2,1)S(1)}, bf16[4,1024]{1,0:T(4,128)(2,1)S(1)}, u32[]{:S(2)}, u32[]{:S(2)}) %collective-permute-start.4) | collective-permute-done | bytes 8224 | tf_op jit(solution)/shard_map/ppermute | solution.py:64
  44.3 7.2 %collective-permute-done.5 = bf16[4,1024]{1,0:T(4,128)(2,1)S(1)} collective-permute-done((bf16[4,1024]{1,0:T(4,128)(2,1)S(1)}, bf16[4,1024]{1,0:T(4,128)(2,1)S(1)}, u32[]{:S(2)}, u32[]{:S(2)}) %collective-permute-start.5) | collective-permute-done | bytes 8224 | tf_op jit(solution)/shard_map/ppermute | solution.py:64
  51.6 7.2 %collective-permute-done.6 = bf16[4,1024]{1,0:T(4,128)(2,1)S(1)} collective-permute-done((bf16[4,1024]{1,0:T(4,128)(2,1)S(1)}, bf16[4,1024]{1,0:T(4,128)(2,1)S(1)}, u32[]{:S(2)}, u32[]{:S(2)}) %collective-permute-start.6) | collective-permute-done | bytes 8224 | tf_op jit(solution)/shard_map/ppermute | solution.py:64
  59.7 6.4 %collective-permute-done.7 = bf16[4,1024]{1,0:T(4,128)(2,1)S(1)} collective-permute-done((bf16[4,1024]{1,0:T(4,128)(2,1)S(1)}, bf16[4,1024]{1,0:T(4,128)(2,1)S(1)}, u32[]{:S(2)}, u32[]{:S(2)}) %collective-permute-start.7) | collective-permute-done | bytes 8224 | tf_op jit(solution)/shard_map/ppermute | solution.py:64
  66.8 6.5 %collective-permute-done.8 = bf16[4,1024]{1,0:T(4,128)(2,1)S(1)} collective-permute-done((bf16[4,1024]{1,0:T(4,128)(2,1)S(1)}, bf16[4,1024]{1,0:T(4,128)(2,1)S(1)}, u32[]{:S(2)}, u32[]{:S(2)}) %collective-permute-start.8) | collective-permute-done | bytes 8224 | tf_op jit(solution)/shard_map/ppermute | solution.py:64
  73.3 7.2 %collective-permute-done.9 = bf16[4,1024]{1,0:T(4,128)(2,1)S(1)} collective-permute-done((bf16[4,1024]{1,0:T(4,128)(2,1)S(1)}, bf16[4,1024]{1,0:T(4,128)(2,1)S(1)}, u32[]{:S(2)}, u32[]{:S(2)}) %collective-permute-start.9) | collective-permute-done | bytes 8224 | tf_op jit(solution)/shard_map/ppermute | solution.py:64
  80.6 4.4 %select_reduce_fusion = (pred[1536]{0:T(1024)(128)(4,1)S(1)}, pred[1536]{0:T(1024)(128)(4,1)S(1)}, pred[1536]{0:T(1024)(128)(4,1)S(1)}, pred[1536]{0:T(1024)(128...) fusion(pred[]{:T(512)} %bitcast.11, pred[]{:T(512)} %bitcast.12, pred[]{:T(512)} %bitcast.13, ...), kind=kLoop, calls=%fused_computation.26 | loop fusion | flops 29184 | bytes 21511 | tf_op jit(solution)/shard_map/while/body/eval_jaxpr/jit(_take)/gather | solution.py:84
  85.0 2.8 %collective-permute-done.10 = bf16[4,1024]{1,0:T(4,128)(2,1)S(1)} collective-permute-done((bf16[4,1024]{1,0:T(4,128)(2,1)S(1)}, bf16[4,1024]{1,0:T(4,128)(2,1)S(1)}, u32[]{:S(2)}, u32[]{:S(2)}) %collective-permute-start.10) | collective-permute-done | bytes 8224 | tf_op jit(solution)/shard_map/ppermute | solution.py:64
  87.8 3.2 %fusion.27 = pred[1536]{0:T(1024)(128)(4,1)S(1)} fusion(pred[1536]{0:T(1024)(128)(4,1)S(1)} %get-tuple-element.253, pred[1536]{0:T(1024)(128)(4,1)S(1)} %get-tuple-element.252, pred[1536]{0:T(1024)(128)(4,1)S(1)} %get-tuple-element.251, pred[1536]{0:T(1024)(128)(4,1)S(1)} %get-tuple-element.249, pred[1536]{0:T(1024)(128)(4,1)S(1)} %get-tuple-element.250, ...), kind=kLoop, calls=%fused_computation.45 | loop fusion | flops 21504 | bytes 10757 | tf_op jit(solution)/shard_map/while/body/eval_jaxpr/jit(_take)/select_n | solution.py:84
  91.0 4.0 %collective-permute-done.11 = bf16[4,1024]{1,0:T(4,128)(2,1)S(1)} collective-permute-done((bf16[4,1024]{1,0:T(4,128)(2,1)S(1)}, bf16[4,1024]{1,0:T(4,128)(2,1)S(1)}, u32[]{:S(2)}, u32[]{:S(2)}) %collective-permute-start.11) | collective-permute-done | bytes 8224 | tf_op jit(solution)/shard_map/ppermute | solution.py:64
  95.1 7.2 %collective-permute-done.12 = bf16[4,1024]{1,0:T(4,128)(2,1)S(1)} collective-permute-done((bf16[4,1024]{1,0:T(4,128)(2,1)S(1)}, bf16[4,1024]{1,0:T(4,128)(2,1)S(1)}, u32[]{:S(2)}, u32[]{:S(2)}) %collective-permute-start.12) | collective-permute-done | bytes 8224 | tf_op jit(solution)/shard_map/ppermute | solution.py:64
  102.3 7.2 %collective-permute-done.13 = bf16[4,1024]{1,0:T(4,128)(2,1)S(1)} collective-permute-done((bf16[4,1024]{1,0:T(4,128)(2,1)S(1)}, bf16[4,1024]{1,0:T(4,128)(2,1)S(1)}, u32[]{:S(2)}, u32[]{:S(2)}) %collective-permute-start.13) | collective-permute-done | bytes 8224 | tf_op jit(solution)/shard_map/ppermute | solution.py:64
  109.7 7.1 %collective-permute-done.14 = bf16[4,1024]{1,0:T(4,128)(2,1)S(1)} collective-permute-done((bf16[4,1024]{1,0:T(4,128)(2,1)S(1)}, bf16[4,1024]{1,0:T(4,128)(2,1)S(1)}, u32[]{:S(2)}, u32[]{:S(2)}) %collective-permute-start.14) | collective-permute-done | bytes 8224 | tf_op jit(solution)/shard_map/ppermute | solution.py:64
  116.8 1.9 concatenate.12
  118.8 2.0 fusion.36
  120.8 1.5 fusion.12
  123.3 36.3 %all-gather.4 = f32[16,64,8]{1,2,0:T(8,128)S(1)} all-gather(f32[1,64,8]{1,2,0:T(8,128)S(1)} %copy.27), channel_id=3, replica_groups=mesh['groups'=1,'kcol'=16,'qrow'=2] {'kcol'}, dimensions={0}, use_global_device_ids=true | all-gather | bytes 34816 | tf_op jit(solution)/shard_map/all_gather | solution.py:12
  159.6 39.1 %all-gather.3 = f32[16,64,8]{1,2,0:T(8,128)S(1)} all-gather(f32[1,64,8]{1,2,0:T(8,128)S(1)} %copy.26), channel_id=2, replica_groups=mesh['groups'=1,'kcol'=16,'qrow'=2] {'kcol'}, dimensions={0}, use_global_device_ids=true | all-gather | bytes 34816 | tf_op jit(solution)/shard_map/all_gather | solution.py:12
  199.7 21.3 %while.26 = (s32[]{:T(128)}, f32[64,8]{0,1:T(8,128)S(1)}, f32[64,8]{0,1:T(8,128)S(1)}, f32[64,8,128]{2,1,0:T(8,128)S(1)}, f32[16,64,8]{1,2,0:T(8,128)S(1)}, /*in...) while((s32[]{:T(128)}, f32[64,8]{0,1:T(8,128)S(1)}, ...), condition=%wide.region_4.5_spmd, body=%wide.region_3.4_spmd.sunk | while | flops 199685 | bytes 815247 | solution.py:17
  (98 shorter events, 25.5 us)
Async XLA Ops:
  6.5 192.2 %all-gather.7.cloned.1.call-start = ((), (), s32[]{:S(2)}) async-start(), calls=%async_computation | async-start | bytes 4456448 | tf_op jit(solution)/shard_map/all_gather | solution.py:12
  6.5 8.8 %collective-permute-start = (bf16[4,1024]{1,0:T(4,128)(2,1)}, bf16[4,1024]{1,0:T(4,128)(2,1)S(1)}, u32[]{:S(2)}, u32[]{:S(2)}) collective-permute-start(bf16[4,1024]{1,0:T(4,128)(2,1)} %param.7), channel_id=1, source_target_pairs={{0,2},{2,4},{4,6},{6,8},{8,10},{10,12},{12,14},{14,16},{16,18},{18... | collective-permute-start | bytes 24584 | tf_op jit(solution)/shard_map/ppermute | solution.py:64
  15.3 7.2 %collective-permute-start.1 = (bf16[4,1024]{1,0:T(4,128)(2,1)S(1)}, bf16[4,1024]{1,0:T(4,128)(2,1)S(1)}, u32[]{:S(2)}, u32[]{:S(2)}) collective-permute-start(bf16[4,1024]{1,0:T(4,128)(2,1)S(1)} %collective-permute-done), channel_id=1, source_target_pairs={{0,2},{2,4},{4,6},{6,8},{8,10},{10,12},{12,14},{14,16},{16,18},{18... | collective-permute-start | bytes 24584 | tf_op jit(solution)/shard_map/ppermute | solution.py:64
  22.6 7.2 %collective-permute-start.2 = (bf16[4,1024]{1,0:T(4,128)(2,1)S(1)}, bf16[4,1024]{1,0:T(4,128)(2,1)S(1)}, u32[]{:S(2)}, u32[]{:S(2)}) collective-permute-start(bf16[4,1024]{1,0:T(4,128)(2,1)S(1)} %collective-permute-done.1), channel_id=1, source_target_pairs={{0,2},{2,4},{4,6},{6,8},{8,10},{10,12},{12,14},{14,16},{16,18},{18... | collective-permute-start | bytes 24584 | tf_op jit(solution)/shard_map/ppermute | solution.py:64
  29.8 7.2 %collective-permute-start.3 = (bf16[4,1024]{1,0:T(4,128)(2,1)S(1)}, bf16[4,1024]{1,0:T(4,128)(2,1)S(1)}, u32[]{:S(2)}, u32[]{:S(2)}) collective-permute-start(bf16[4,1024]{1,0:T(4,128)(2,1)S(1)} %collective-permute-done.2), channel_id=1, source_target_pairs={{0,2},{2,4},{4,6},{6,8},{8,10},{10,12},{12,14},{14,16},{16,18},{18... | collective-permute-start | bytes 24584 | tf_op jit(solution)/shard_map/ppermute | solution.py:64
  37.1 7.2 %collective-permute-start.4 = (bf16[4,1024]{1,0:T(4,128)(2,1)S(1)}, bf16[4,1024]{1,0:T(4,128)(2,1)S(1)}, u32[]{:S(2)}, u32[]{:S(2)}) collective-permute-start(bf16[4,1024]{1,0:T(4,128)(2,1)S(1)} %collective-permute-done.3), channel_id=1, source_target_pairs={{0,2},{2,4},{4,6},{6,8},{8,10},{10,12},{12,14},{14,16},{16,18},{18... | collective-permute-start | bytes 24584 | tf_op jit(solution)/shard_map/ppermute | solution.py:64
  44.3 7.2 %collective-permute-start.5 = (bf16[4,1024]{1,0:T(4,128)(2,1)S(1)}, bf16[4,1024]{1,0:T(4,128)(2,1)S(1)}, u32[]{:S(2)}, u32[]{:S(2)}) collective-permute-start(bf16[4,1024]{1,0:T(4,128)(2,1)S(1)} %collective-permute-done.4), channel_id=1, source_target_pairs={{0,2},{2,4},{4,6},{6,8},{8,10},{10,12},{12,14},{14,16},{16,18},{18... | collective-permute-start | bytes 24584 | tf_op jit(solution)/shard_map/ppermute | solution.py:64
  51.6 7.2 %collective-permute-start.6 = (bf16[4,1024]{1,0:T(4,128)(2,1)S(1)}, bf16[4,1024]{1,0:T(4,128)(2,1)S(1)}, u32[]{:S(2)}, u32[]{:S(2)}) collective-permute-start(bf16[4,1024]{1,0:T(4,128)(2,1)S(1)} %collective-permute-done.5), channel_id=1, source_target_pairs={{0,2},{2,4},{4,6},{6,8},{8,10},{10,12},{12,14},{14,16},{16,18},{18... | collective-permute-start | bytes 24584 | tf_op jit(solution)/shard_map/ppermute | solution.py:64
  58.8 7.2 %collective-permute-start.7 = (bf16[4,1024]{1,0:T(4,128)(2,1)S(1)}, bf16[4,1024]{1,0:T(4,128)(2,1)S(1)}, u32[]{:S(2)}, u32[]{:S(2)}) collective-permute-start(bf16[4,1024]{1,0:T(4,128)(2,1)S(1)} %collective-permute-done.6), channel_id=1, source_target_pairs={{0,2},{2,4},{4,6},{6,8},{8,10},{10,12},{12,14},{14,16},{16,18},{18... | collective-permute-start | bytes 24584 | tf_op jit(solution)/shard_map/ppermute | solution.py:64
  66.1 7.2 %collective-permute-start.8 = (bf16[4,1024]{1,0:T(4,128)(2,1)S(1)}, bf16[4,1024]{1,0:T(4,128)(2,1)S(1)}, u32[]{:S(2)}, u32[]{:S(2)}) collective-permute-start(bf16[4,1024]{1,0:T(4,128)(2,1)S(1)} %collective-permute-done.7), channel_id=1, source_target_pairs={{0,2},{2,4},{4,6},{6,8},{8,10},{10,12},{12,14},{14,16},{16,18},{18... | collective-permute-start | bytes 24584 | tf_op jit(solution)/shard_map/ppermute | solution.py:64
  73.3 7.2 %collective-permute-start.9 = (bf16[4,1024]{1,0:T(4,128)(2,1)S(1)}, bf16[4,1024]{1,0:T(4,128)(2,1)S(1)}, u32[]{:S(2)}, u32[]{:S(2)}) collective-permute-start(bf16[4,1024]{1,0:T(4,128)(2,1)S(1)} %collective-permute-done.8), channel_id=1, source_target_pairs={{0,2},{2,4},{4,6},{6,8},{8,10},{10,12},{12,14},{14,16},{16,18},{18... | collective-permute-start | bytes 24584 | tf_op jit(solution)/shard_map/ppermute | solution.py:64
  80.6 7.2 %collective-permute-start.10 = (bf16[4,1024]{1,0:T(4,128)(2,1)S(1)}, bf16[4,1024]{1,0:T(4,128)(2,1)S(1)}, u32[]{:S(2)}, u32[]{:S(2)}) collective-permute-start(bf16[4,1024]{1,0:T(4,128)(2,1)S(1)} %collective-permute-done.9), channel_id=1, source_target_pairs={{0,2},{2,4},{4,6},{6,8},{8,10},{10,12},{12,14},{14,16},{16,18},{18... | collective-permute-start | bytes 24584 | tf_op jit(solution)/shard_map/ppermute | solution.py:64
  87.8 7.2 %collective-permute-start.11 = (bf16[4,1024]{1,0:T(4,128)(2,1)S(1)}, bf16[4,1024]{1,0:T(4,128)(2,1)S(1)}, u32[]{:S(2)}, u32[]{:S(2)}) collective-permute-start(bf16[4,1024]{1,0:T(4,128)(2,1)S(1)} %collective-permute-done.10), channel_id=1, source_target_pairs={{0,2},{2,4},{4,6},{6,8},{8,10},{10,12},{12,14},{14,16},{16,18},{18... | collective-permute-start | bytes 24584 | tf_op jit(solution)/shard_map/ppermute | solution.py:64
  95.1 7.2 %collective-permute-start.12 = (bf16[4,1024]{1,0:T(4,128)(2,1)S(1)}, bf16[4,1024]{1,0:T(4,128)(2,1)S(1)}, u32[]{:S(2)}, u32[]{:S(2)}) collective-permute-start(bf16[4,1024]{1,0:T(4,128)(2,1)S(1)} %collective-permute-done.11), channel_id=1, source_target_pairs={{0,2},{2,4},{4,6},{6,8},{8,10},{10,12},{12,14},{14,16},{16,18},{18... | collective-permute-start | bytes 24584 | tf_op jit(solution)/shard_map/ppermute | solution.py:64
  102.3 7.2 %collective-permute-start.13 = (bf16[4,1024]{1,0:T(4,128)(2,1)S(1)}, bf16[4,1024]{1,0:T(4,128)(2,1)S(1)}, u32[]{:S(2)}, u32[]{:S(2)}) collective-permute-start(bf16[4,1024]{1,0:T(4,128)(2,1)S(1)} %collective-permute-done.12), channel_id=1, source_target_pairs={{0,2},{2,4},{4,6},{6,8},{8,10},{10,12},{12,14},{14,16},{16,18},{18... | collective-permute-start | bytes 24584 | tf_op jit(solution)/shard_map/ppermute | solution.py:64
  109.6 7.2 %collective-permute-start.14 = (bf16[4,1024]{1,0:T(4,128)(2,1)S(1)}, bf16[4,1024]{1,0:T(4,128)(2,1)S(1)}, u32[]{:S(2)}, u32[]{:S(2)}) collective-permute-start(bf16[4,1024]{1,0:T(4,128)(2,1)S(1)} %collective-permute-done.13), channel_id=1, source_target_pairs={{0,2},{2,4},{4,6},{6,8},{8,10},{10,12},{12,14},{14,16},{16,18},{18... | collective-permute-start | bytes 24584 | tf_op jit(solution)/shard_map/ppermute | solution.py:64
  118.7 2.1 copy-start
Sparse Core Ops, SparseCore 0:
  122.4 72.0 all-gather.6
